TPU v7x, 128 devices: a whole 4x4x4 slice. The times are simulated.
128 devices in a mesh: rows: 32 (over x, z, core), modes: 4 (over y).
Axes of the slice: x: 4, y: 4, z: 4, core: 2. Of those that a mesh axis runs over, the one named last changes fastest.
Arguments:
- activations: bfloat16 [2048, 64, 2048], P('rows', None, 'modes'), may hold values from -6 to 6
- cotangent: bfloat16 [2048, 64, 2048], P('rows', None, 'modes'), may hold values from -6 to 6
- spectral_weight: bfloat16 [64, 64, 64, 128], P('rows', None, None, 'modes'), may hold values from -12 to 12
- linear_weight: bfloat16 [64, 64], replicated, may hold values from -0.75 to 0.75
- bias: float32 [64], replicated, may hold values from -4 to 4
Outputs:
- grad_input: bfloat16 [2048, 64, 2048], P('rows', None, 'modes')
- grad_spectral: float32 [64, 64, 64, 128], P('rows', None, None, 'modes')
- grad_linear: float32 [64, 64], replicated
- grad_bias: float32 [64], replicated
All inputs are finite; a program needn't handle non-finite values.
Results may differ from a plain program's by a relative error of at most 0.03.
Values may be sent and summed in bfloat16 or wider, within the bound.
A program may use at most 128 MiB of HBM per device.

v0:
```python
import math
import jax
import jax.numpy as jnp
from jax import lax
from jax.sharding import PartitionSpec as P

HIGHEST_PRECISION = lax.Precision.HIGHEST


def row_angles(freq_count, row_start, row_count, period):
    positions = jnp.arange(freq_count, dtype=jnp.int32)
    frequency = jnp.where(positions < freq_count // 2, positions, positions - freq_count)
    grid_rows = row_start + jnp.arange(row_count, dtype=jnp.int32)
    phases = frequency[:, None] * grid_rows[None, :] % period
    angles = phases.astype(jnp.float32) * (2.0 * math.pi / period)
    return (jnp.cos(angles), jnp.sin(angles))


def column_table(mode_count, col_start, col_count, period):
    mode_ids = jnp.arange(mode_count, dtype=jnp.int32)
    grid_cols = col_start + jnp.arange(col_count, dtype=jnp.int32)
    phases = grid_cols[:, None] * mode_ids[None, :] % period
    angles = phases.astype(jnp.float32) * (2.0 * math.pi / period)
    return jnp.stack([jnp.cos(angles), -jnp.sin(angles)], axis=-1).reshape(
        col_count, 2 * mode_count
    )


def column_weights(mode_count):
    mode_ids = jnp.arange(mode_count, dtype=jnp.int32)
    return jnp.repeat(jnp.where(mode_ids == 0, 1.0, 2.0).astype(jnp.float32), 2)


def to_freq(values, cos_rows, sin_rows):
    length = cos_rows.shape[0]
    stacked = jnp.concatenate([cos_rows, sin_rows], axis=0)
    product = jnp.dot(
        stacked,
        values.reshape(values.shape[0], -1),
        precision=HIGHEST_PRECISION,
        preferred_element_type=jnp.float32,
    )
    halves = product.reshape(2, length, values.shape[1], values.shape[2] // 2, 2)
    real_part = halves[0, ..., 0] + halves[1, ..., 1]
    imag_part = halves[0, ..., 1] - halves[1, ..., 0]
    return jnp.stack([real_part, imag_part], axis=-1).reshape(
        length, values.shape[1], values.shape[2]
    )


def to_rows(values, cos_cols, sin_cols):
    length = cos_cols.shape[0]
    stacked = jnp.concatenate([cos_cols, sin_cols], axis=0)
    product = jnp.dot(
        stacked, values.reshape(values.shape[0], -1), preferred_element_type=jnp.float32
    )
    halves = product.reshape(2, length, values.shape[1], values.shape[2] // 2, 2)
    real_part = halves[0, ..., 0] - halves[1, ..., 1]
    imag_part = halves[0, ..., 1] + halves[1, ..., 0]
    return jnp.stack([real_part, imag_part], axis=-1).reshape(
        length, values.shape[1], values.shape[2]
    )


def gelu_grad(preact):
    cumulative = 0.5 * (1.0 + jax.scipy.special.erf(preact * 0.7071067811865476))
    density = jnp.exp(-0.5 * preact * preact) * 0.3989422804014327
    return cumulative + preact * density


def body(activations, cotangent, spectral_weight, linear_weight, bias):
    rows_here, channels, cols_here = activations.shape
    row_devices = lax.axis_size("rows")
    mode_devices = lax.axis_size("modes")
    row_index = lax.axis_index("rows")
    mode_index = lax.axis_index("modes")
    grid_rows = rows_here * row_devices
    grid_cols = cols_here * mode_devices
    kept_rows = spectral_weight.shape[0]
    block_cols = spectral_weight.shape[3]
    freq_rows = kept_rows * row_devices
    spec_cols = block_cols * mode_devices
    inv_area = 1.0 / (grid_rows * grid_cols)
    forward_table = column_table(spec_cols // 2, mode_index * cols_here, cols_here, grid_cols)
    analysis = forward_table.astype(jnp.bfloat16)
    synthesis = (forward_table.T * column_weights(spec_cols // 2)[:, None]).astype(jnp.bfloat16)
    cos_rows, sin_rows = row_angles(freq_rows, row_index * rows_here, rows_here, grid_rows)
    cos_cols = cos_rows.T.astype(jnp.bfloat16)
    sin_cols = sin_rows.T.astype(jnp.bfloat16)

    def reduce_spectrum(term):
        arranged = term.reshape(row_devices, kept_rows, channels, mode_devices, block_cols)
        arranged = arranged.transpose(0, 3, 1, 2, 4).reshape(
            row_devices * mode_devices * kept_rows, channels, block_cols
        )
        return lax.psum_scatter(arranged, ("rows", "modes"), scatter_dimension=0, tiled=True)

    def expand_spectrum(spectrum):
        gathered = lax.all_gather(spectrum, ("rows", "modes"), axis=0, tiled=True)
        arranged = gathered.reshape(row_devices, mode_devices, kept_rows, channels, block_cols)
        arranged = arranged.transpose(0, 2, 3, 1, 4).reshape(freq_rows, channels, spec_cols)
        return to_rows(arranged, cos_cols, sin_cols).astype(jnp.bfloat16)

    partial_cols = jnp.einsum(
        "hcw,wq->hcq", activations, analysis, preferred_element_type=jnp.float32
    )
    spectrum = reduce_spectrum(to_freq(partial_cols, cos_rows, sin_rows)).astype(jnp.bfloat16)
    parts = spectrum.reshape(kept_rows, channels, block_cols // 2, 2)
    wparts = spectral_weight.reshape(kept_rows, channels, channels, block_cols // 2, 2)
    spec_re = parts[..., 0]
    spec_im = parts[..., 1]
    weight_re = wparts[..., 0]
    weight_im = wparts[..., 1]
    mixed_re = jnp.einsum(
        "kcm,kcom->kom", spec_re, weight_re, preferred_element_type=jnp.float32
    ) - jnp.einsum("kcm,kcom->kom", spec_im, weight_im, preferred_element_type=jnp.float32)
    mixed_im = jnp.einsum(
        "kcm,kcom->kom", spec_re, weight_im, preferred_element_type=jnp.float32
    ) + jnp.einsum("kcm,kcom->kom", spec_im, weight_re, preferred_element_type=jnp.float32)
    mixed = (
        jnp.stack([mixed_re, mixed_im], axis=-1)
        .reshape(kept_rows, channels, block_cols)
        .astype(jnp.bfloat16)
    )
    rowfield = expand_spectrum(mixed)
    spectral = (
        jnp.einsum("hcq,qw->hcw", rowfield, synthesis, preferred_element_type=jnp.float32)
        * inv_area
    )
    linear = jnp.einsum(
        "hcw,co->how", activations, linear_weight, preferred_element_type=jnp.float32
    )
    preact = spectral + linear + bias[None, :, None]
    dpre = (cotangent.astype(jnp.float32) * gelu_grad(preact)).astype(jnp.bfloat16)
    grad_lin_part = jnp.einsum("hcw,how->co", activations, dpre, preferred_element_type=jnp.float32)
    grad_bias_part = jnp.sum(dpre.astype(jnp.float32), axis=(0, 2))
    grad_lin_sum, grad_bias_sum = lax.psum((grad_lin_part, grad_bias_part), ("rows", "modes"))
    dpartial = (
        jnp.einsum("hcw,qw->hcq", dpre, synthesis, preferred_element_type=jnp.float32) * inv_area
    )
    dmixed = reduce_spectrum(to_freq(dpartial, cos_rows, sin_rows)).astype(jnp.bfloat16)
    dparts = dmixed.reshape(kept_rows, channels, block_cols // 2, 2)
    dmix_re = dparts[..., 0]
    dmix_im = dparts[..., 1]
    spec_re_wide = spec_re.astype(jnp.float32)
    spec_im_wide = spec_im.astype(jnp.float32)
    dmix_re_wide = dmix_re.astype(jnp.float32)
    dmix_im_wide = dmix_im.astype(jnp.float32)
    grad_real = (
        spec_re_wide[:, :, None, :] * dmix_re_wide[:, None, :, :]
        + spec_im_wide[:, :, None, :] * dmix_im_wide[:, None, :, :]
    )
    grad_imag = (
        spec_re_wide[:, :, None, :] * dmix_im_wide[:, None, :, :]
        - spec_im_wide[:, :, None, :] * dmix_re_wide[:, None, :, :]
    )
    grad_spectral = jnp.stack([grad_real, grad_imag], axis=-1).reshape(
        kept_rows, channels, channels, block_cols
    )
    dspec_re = jnp.einsum(
        "kcom,kom->kcm", weight_re, dmix_re, preferred_element_type=jnp.float32
    ) + jnp.einsum("kcom,kom->kcm", weight_im, dmix_im, preferred_element_type=jnp.float32)
    dspec_im = jnp.einsum(
        "kcom,kom->kcm", weight_re, dmix_im, preferred_element_type=jnp.float32
    ) - jnp.einsum("kcom,kom->kcm", weight_im, dmix_re, preferred_element_type=jnp.float32)
    dspectrum = (
        jnp.stack([dspec_re, dspec_im], axis=-1)
        .reshape(kept_rows, channels, block_cols)
        .astype(jnp.bfloat16)
    )
    drows = expand_spectrum(dspectrum)
    spectral_part = jnp.einsum("hcq,wq->hcw", drows, analysis, preferred_element_type=jnp.float32)
    local_part = jnp.einsum("how,co->hcw", dpre, linear_weight, preferred_element_type=jnp.float32)
    grad_input = (spectral_part + local_part).astype(jnp.bfloat16)
    return (grad_input, grad_spectral, grad_lin_sum / grid_rows, grad_bias_sum / grid_rows)


def solution(mesh):
    return jax.shard_map(
        body,
        mesh=mesh,
        in_specs=(
            P("rows", None, "modes"),
            P("rows", None, "modes"),
            P("rows", None, None, "modes"),
            P(),
            P(),
        ),
        out_specs=(P("rows", None, "modes"), P("rows", None, None, "modes"), P(), P()),
        check_vma=False,
    )
```

profile of v0, /device:TPU:1, one launch (start us, length us, event | category | flops | bytes accessed | tf_op | source)
XLA Modules:
  0.0 1558.9 jit_solution(16695946387777610892)
XLA Ops:
  7.3 0.5 fusion.58
  7.8 0.6 copy-done.3
  9.0 3.4 convolution_bitcast_fusion
  12.4 2.8 copy.152
  15.6 0.6 copy-done.8
  16.2 14.0 fusion.10
  30.2 0.6 fusion.23
  30.7 0.6 fusion.25
  31.3 2.5 pad_maximum_fusion
  33.8 7.2 copy.98
  41.0 4.9 copy.99
  46.0 1.1 copy-done.5
  47.2 0.4 copy.100
  47.6 636.6 %reduce-scatter.3.cloned.1.call-done = f32[2,64,32]{1,2,0:T(8,128)} async-done(((f32[256,64,32]{1,2,0:T(8,128)}), f32[2,64,32]{1,2,0:T(8,128)}) %reduce-scatter.3.cloned.1.call-update) | async-done | bytes 16400 | tf_op jit(solution)/shard_map/reduce_scatter | solution.py:96
  684.1 0.8 convert_element_type.104
  685.9 0.6 copy.103
  686.6 0.6 reduce-scatter.5.cloned.1.call-start
  687.2 0.7 mul.222
  687.9 0.6 pad_maximum_fusion.7
  688.5 67.7 %all-gather.3.cloned.1.call-done = bf16[256,64,32]{1,2,0:T(8,128)(2,1)} async-done(((bf16[2,64,32]{1,2,0:T(8,128)(2,1)}), bf16[256,64,32]{1,2,0:T(8,128)(2,1)}) %all-gather.3.cloned.1.call-update) | async-done | bytes 1048592 | tf_op jit(solution)/shard_map/all_gather | solution.py:99
  756.2 6.9 copy.104
  763.1 5.9 reshape_reshape.13
  769.0 1.1 copy.105
  770.1 2.9 fusion.28
  772.9 0.5 fusion.35
  773.4 0.5 fusion.36
  773.9 0.5 pad_maximum_fusion.2
  774.4 3.7 copy.109
  778.1 4.3 fusion.32
  782.5 6.0 convert_reduce_fusion
  788.5 2.0 copy-done.1
  790.5 1.3 convolution_multiply_fusion
  791.9 2.7 copy.158
  794.6 14.1 fusion.8
  808.7 0.6 fusion.17
  809.3 0.6 fusion.19
  809.8 2.4 pad_maximum_fusion.1
  812.3 7.3 copy.118
  819.6 4.8 copy.119
  824.5 0.6 copy-done.12
  825.4 4.8 convolution_bitcast_fusion.1
  830.1 64.0 %all-reduce = (f32[64,64]{0,1:T(8,128)S(1)}, f32[64]{0:T(128)S(1)}) all-reduce(f32[64,64]{0,1:T(8,128)S(1)} %convolution_bitcast_fusion.1, f32[64]{0:T(128)S(1)} %get-tuple-element.34), channel_id=1, replica_groups=mesh['rows'=32,'modes'=4] {'rows','modes'}, use_global_device_ids=true, to_apply=%region_2.3 | all-reduce | flops 4160 | bytes 33280 | tf_op jit(solution)/shard_map/psum | solution.py:137
  894.1 0.7 copy.129
  894.8 563.3 %reduce-scatter.5.cloned.1.call-done = f32[2,64,32]{1,2,0:T(8,128)} async-done(((f32[256,64,32]{1,2,0:T(8,128)}), f32[2,64,32]{1,2,0:T(8,128)}) %reduce-scatter.5.cloned.1.call-update) | async-done | bytes 16400 | tf_op jit(solution)/shard_map/reduce_scatter | solution.py:96
  1458.1 0.8 convert_element_type.109
  1458.9 0.4 fusion.43
  1459.2 0.4 fusion.39
  1459.6 0.4 fusion.44
  1460.0 0.4 fusion.40
  1460.4 0.6 copy.120
  1461.1 0.5 broadcast_multiply_fusion.1
  1461.6 6.7 fusion.67
  1468.4 5.0 multiply_add_fusion
  1473.3 3.6 pad_maximum_fusion.4
  1476.9 52.4 %all-gather.5.cloned.1.call-done = bf16[256,64,32]{1,2,0:T(8,128)(2,1)} async-done(((bf16[2,64,32]{1,2,0:T(8,128)(2,1)}), bf16[256,64,32]{1,2,0:T(8,128)(2,1)}) %all-gather.5.cloned.1.call-update) | async-done | bytes 1048592 | tf_op jit(solution)/shard_map/all_gather | solution.py:99
  1529.3 6.9 copy.121
  1536.2 5.9 reshape_reshape.15
  1542.1 1.3 copy.122
  1543.5 2.3 fusion.26
  1545.8 0.5 fusion.37
  1546.3 0.5 fusion.38
  1546.7 0.5 pad_maximum_fusion.3
  1547.2 0.7 slice-done.1
  1548.1 4.1 fusion.6
  (67 shorter events, 2.6 us)
Async XLA Ops:
  7.2 775.3 %copy-start = (bf16[64,64]{1,0:T(8,128)(2,1)S(1)}, bf16[64,64]{1,0:T(8,128)(2,1)}, u32[]{:S(2)}) copy-start(bf16[64,64]{1,0:T(8,128)(2,1)} %param.8) | copy-start | bytes 24580
  7.2 677.0 %reduce-scatter.3.cloned.1.call-start = ((), (), s32[]{:S(2)}) async-start(), calls=%async_computation.2 | async-start | bytes 4227072 | tf_op jit(solution)/shard_map/reduce_scatter | solution.py:96
  7.8 0.6 copy-start.3
  15.6 0.6 copy-start.8
  45.9 1.2 copy-start.5
  46.0 710.2 %all-gather.3.cloned.1.call-start = ((), (), s32[]{:S(2)}) async-start(), calls=%async_computation.3 | async-start | bytes 2113536 | tf_op jit(solution)/shard_map/all_gather | solution.py:99
  47.6 715.5 %copy-start.6 = (bf16[2,64,64,32]{2,1,3,0:T(8,128)(2,1)}, bf16[2,64,64,32]{2,1,3,0:T(8,128)(2,1)S(1)}, u32[]{:S(2)}) copy-start(bf16[2,64,64,32]{2,1,3,0:T(8,128)(2,1)S(1)} %copy.100) | copy-start | bytes 1572868
  684.9 78.2 %copy-start.11 = (bf16[2,64,32]{1,2,0:T(8,128)(2,1)}, bf16[2,64,32]{1,2,0:T(8,128)(2,1)S(1)}, u32[]{:S(2)}) copy-start(bf16[2,64,32]{1,2,0:T(8,128)(2,1)S(1)} %convert_element_type.104) | copy-start | bytes 24580
  686.6 771.5 %reduce-scatter.5.cloned.1.call-start = ((), (), s32[]{:S(2)}) async-start(), calls=%async_computation.4 | async-start | bytes 4227072 | tf_op jit(solution)/shard_map/reduce_scatter | solution.py:96
  773.9 4.2 copy-start.13
  778.1 4.3 copy-start.2
  778.1 4.4 copy-start.14
  778.1 4.4 copy-start.15
  788.5 2.0 copy-start.1
  791.9 2.7 copy-start.9
  824.4 0.7 copy-start.12
  824.4 704.9 %all-gather.5.cloned.1.call-start = ((), (), s32[]{:S(2)}) async-start(), calls=%async_computation.5 | async-start | bytes 2113536 | tf_op jit(solution)/shard_map/all_gather | solution.py:99
  825.3 633.5 %copy-start.7 = (bf16[2,64,64,32]{2,1,3,0:T(8,128)(2,1)S(1)}, bf16[2,64,64,32]{2,1,3,0:T(8,128)(2,1)}, u32[]{:S(2)}) copy-start(bf16[2,64,64,32]{2,1,3,0:T(8,128)(2,1)} %copy-done.6) | copy-start | bytes 1572868
  1536.2 7.2 copy-start.10
  1543.5 3.8 slice-start
  1545.8 2.2 slice-start.1
  1546.3 1.8 copy-start.4
Sparse Core Ops, SparseCore 0:
  46.1 638.0 reduce-scatter.2
  688.1 67.9 all-gather.2
  824.6 633.4 reduce-scatter.4
  1461.2 68.0 all-gather.4
where the time goes:
time: 1570 us; the launch traced here: 1560 us
  waiting for transfers between devices  1320 us (84%)
  local copies, waits for them, and re-layouts  71.3 us (5%)
  matrix products  66.3 us (4%)
  blocking collectives  64 us (4%)
  other arithmetic  22.1 us (1%)
    reduce_scatter x2, waiting for transfers between devices, reduce_spectrum(): lax.psum_scatter(arranged, ('rows', 'modes'), scatter_dimension=0, tiled=...  1200 us
    all_gather x2, waiting for transfers between devices, expand_spectrum(): gathered = lax.all_gather(spectrum, ('rows', 'modes'), axis=0, tiled=True)  120 us
    psum x1, blocking collectives, body(): lax.psum((grad_lin_part, grad_bias_part), ('rows', 'modes'))  64 us
  transfers between devices with their start and end apart: 4, of which 4 were waited for; matrix products, arithmetic and copies ran while one was open for 1% of the time, Pallas kernels for 0%

commit v1 on v0

--- a/solution.py
+++ b/solution.py
@@ -96,7 +96,15 @@
         return lax.psum_scatter(arranged, ("rows", "modes"), scatter_dimension=0, tiled=True)
 
     def expand_spectrum(spectrum):
-        gathered = lax.all_gather(spectrum, ("rows", "modes"), axis=0, tiled=True)
+        inbox = []
+        for _ in range(lax.axis_size(("rows", "modes"))):
+            inbox.append(spectrum)
+        gathered = jnp.concatenate(
+            lax.all_to_all(
+                jnp.stack(inbox, axis=0), axis_name=("rows", "modes"), split_axis=0, concat_axis=0
+            ),
+            0,
+        )
         arranged = gathered.reshape(row_devices, mode_devices, kept_rows, channels, block_cols)
         arranged = arranged.transpose(0, 2, 3, 1, 4).reshape(freq_rows, channels, spec_cols)
         return to_rows(arranged, cos_cols, sin_cols).astype(jnp.bfloat16)

time: 1570 us -> 1490 us (0.949)
  waiting for transfers between devices: 1320 us -> 1220 us
  starting transfers between devices: 0.69 us -> 24.9 us
    all_gather x2 -> x0, waiting for transfers between devices: 120 us -> none  [expand_spectrum(): gathered = lax.all_gather(spectrum, ('rows', 'modes'), axis=0, tiled=True)]
    all_to_all x0 -> x2, waiting for transfers between devices: none -> 29.1 us  [expand_spectrum(): lax.all_to_all(jnp.stack(inbox, axis=0), axis_name=('rows', 'modes'), spl...]
    all_to_all x0 -> x2, starting transfers between devices: none -> 24.8 us  [expand_spectrum(): lax.all_to_all(jnp.stack(inbox, axis=0), axis_name=('rows', 'modes'), spl...]
  transfers between devices with their start and end apart: 4 -> 4, of which waited for: 4 -> 4; matrix products, arithmetic and copies ran while one was open for 1% -> 2% of each run, Pallas kernels for 0% -> 0%
where the time goes in v1:
time: 1490 us
  waiting for transfers between devices  1220 us (82%)
  local copies, waits for them, and re-layouts  74.2 us (5%)
  matrix products  66.8 us (4%)
  blocking collectives  63.9 us (4%)
  starting transfers between devices  24.9 us (2%)
  other arithmetic  23.4 us (2%)
    reduce_scatter x2, waiting for transfers between devices, reduce_spectrum(): lax.psum_scatter(arranged, ('rows', 'modes'), scatter_dimension=0, tiled=...  1190 us
    psum x1, blocking collectives, body(): lax.psum((grad_lin_part, grad_bias_part), ('rows', 'modes'))  63.9 us
  transfers between devices with their start and end apart: 4, of which 4 were waited for; matrix products, arithmetic and copies ran while one was open for 2% of the time, Pallas kernels for 0%

profile of v1, /device:TPU:1, one launch (start us, length us, event | category | flops | bytes accessed | tf_op | source)
XLA Modules:
  0.0 1489.5 jit_solution(10514174604949095116)
XLA Ops:
  7.3 0.5 fusion.58
  7.8 0.6 copy-done.3
  9.0 3.4 convolution_bitcast_fusion
  12.4 3.0 copy.114
  15.4 0.8 fusion.71
  16.3 0.6 copy-done.8
  16.9 13.9 fusion.10
  30.8 0.6 fusion.23
  31.4 0.6 fusion.25
  31.9 2.5 pad_maximum_fusion
  34.4 7.3 copy.60
  41.7 4.9 copy.61
  46.6 1.2 copy-done.5
  48.2 638.2 %reduce-scatter.3.cloned.1.call-done = f32[2,64,32]{1,2,0:T(8,128)} async-done(((f32[256,64,32]{1,2,0:T(8,128)}), f32[2,64,32]{1,2,0:T(8,128)}) %reduce-scatter.3.cloned.1.call-update) | async-done | bytes 16400 | tf_op jit(solution)/shard_map/reduce_scatter | solution.py:96
  686.4 0.8 convert_element_type.108
  688.3 0.5 broadcast_bitcast_fusion.1
  688.8 2.3 reshape.407
  691.1 12.3 all-to-all-start
  703.5 0.7 mul.222
  704.2 1.3 pad_maximum_fusion.7
  705.5 17.8 %all-to-all-done = bf16[128,2,2048]{2,1,0:T(2,128)(2,1)S(1)} async-done(((bf16[128,2,2048]{2,1,0:T(2,128)(2,1)}), bf16[128,2,2048]{2,1,0:T(2,128)(2,1)S(1)}, u32[]{:S(2)}, u32[]{:S(2)}) %all-to-all-start) | async-done | bytes 1048608 | tf_op jit(solution)/shard_map/all_to_all | solution.py:103
  723.3 1.6 reshape.408
  724.9 4.6 copy.66
  729.5 5.9 reshape_reshape.20
  735.4 1.1 copy.67
  736.5 3.1 fusion.28
  739.6 0.5 fusion.35
  740.5 0.5 pad_maximum_fusion.2
  741.0 3.7 copy.71
  744.7 4.3 fusion.32
  749.1 6.0 convert_reduce_fusion
  755.1 2.0 copy-done.1
  757.1 1.3 convolution_multiply_fusion
  758.5 2.8 copy.120
  761.3 14.3 fusion.8
  775.6 0.6 fusion.17
  776.2 0.6 fusion.19
  776.7 2.5 pad_maximum_fusion.1
  779.2 7.2 copy.80
  786.5 5.0 copy.81
  791.5 0.7 copy-done.12
  792.4 4.7 convolution_bitcast_fusion.1
  797.1 63.9 %all-reduce = (f32[64,64]{0,1:T(8,128)S(1)}, f32[64]{0:T(128)S(1)}) all-reduce(f32[64,64]{0,1:T(8,128)S(1)} %convolution_bitcast_fusion.1, f32[64]{0:T(128)S(1)} %get-tuple-element.30), channel_id=1, replica_groups=mesh['rows'=32,'modes'=4] {'rows','modes'}, use_global_device_ids=true, to_apply=%region_2.3 | all-reduce | flops 4160 | bytes 33280 | tf_op jit(solution)/shard_map/psum | solution.py:145
  861.0 0.7 copy.91
  861.7 0.5 broadcast_multiply_fusion.1
  862.2 6.9 fusion.67
  869.0 554.2 %reduce-scatter.5.cloned.1.call-done = f32[2,64,32]{1,2,0:T(8,128)} async-done(((f32[256,64,32]{1,2,0:T(8,128)}), f32[2,64,32]{1,2,0:T(8,128)}) %reduce-scatter.5.cloned.1.call-update) | async-done | bytes 16400 | tf_op jit(solution)/shard_map/reduce_scatter | solution.py:96
  1423.2 0.8 convert_element_type.113
  1425.6 0.5 broadcast_bitcast_fusion
  1426.1 2.3 reshape.409
  1428.4 12.5 all-to-all-start.1
  1441.0 5.0 multiply_add_fusion
  1445.9 3.6 pad_maximum_fusion.4
  1449.5 11.3 all-to-all-done.1
  1460.8 1.4 reshape.410
  1462.2 4.6 copy.83
  1466.9 5.9 reshape_reshape.23
  1472.8 1.1 copy.84
  1473.9 2.3 fusion.26
  1476.2 0.5 fusion.37
  1476.6 0.5 fusion.38
  1477.1 0.5 pad_maximum_fusion.3
  1477.6 0.7 slice-done.1
  1478.4 4.1 fusion.6
  (71 shorter events, 4.6 us)
Async XLA Ops:
  7.2 741.9 %copy-start = (bf16[64,64]{1,0:T(8,128)(2,1)S(1)}, bf16[64,64]{1,0:T(8,128)(2,1)}, u32[]{:S(2)}) copy-start(bf16[64,64]{1,0:T(8,128)(2,1)} %param.8) | copy-start | bytes 24580
  7.2 679.3 %reduce-scatter.3.cloned.1.call-start = ((), (), s32[]{:S(2)}) async-start(), calls=%async_computation.4 | async-start | bytes 4227072 | tf_op jit(solution)/shard_map/reduce_scatter | solution.py:96
  7.8 0.7 copy-start.3
  16.2 0.6 copy-start.8
  46.6 1.2 copy-start.5
  48.2 640.0 %copy-start.6 = (bf16[2,64,64,32]{2,1,3,0:T(8,128)(2,1)}, bf16[2,64,64,32]{2,1,3,0:T(8,128)(2,1)S(1)}, u32[]{:S(2)}) copy-start(bf16[2,64,64,32]{2,1,3,0:T(8,128)(2,1)S(1)} %copy.62) | copy-start | bytes 1572868
  687.2 3.9 copy-start.11
  691.1 32.2 %all-to-all-start = ((bf16[128,2,2048]{2,1,0:T(2,128)(2,1)}), bf16[128,2,2048]{2,1,0:T(2,128)(2,1)S(1)}, u32[]{:S(2)}, u32[]{:S(2)}) async-start(bf16[128,2,2048]{2,1,0:T(2,128)(2,1)} %reshape.407), calls=%async_computation.1 | async-start | bytes 2097152 | tf_op jit(solution)/shard_map/all_to_all | solution.py:103
  703.4 719.8 %reduce-scatter.5.cloned.1.call-start = ((), (), s32[]{:S(2)}) async-start(), calls=%async_computation.5 | async-start | bytes 4227072 | tf_op jit(solution)/shard_map/reduce_scatter | solution.py:96
  740.5 4.2 copy-start.13
  744.7 4.3 copy-start.2
  744.7 4.3 copy-start.14
  744.7 4.4 copy-start.15
  755.1 2.0 copy-start.1
  758.5 2.8 copy-start.9
  791.4 0.7 copy-start.12
  862.2 561.8 %copy-start.7 = (bf16[2,64,64,32]{2,1,3,0:T(8,128)(2,1)S(1)}, bf16[2,64,64,32]{2,1,3,0:T(8,128)(2,1)}, u32[]{:S(2)}) copy-start(bf16[2,64,64,32]{2,1,3,0:T(8,128)(2,1)} %copy-done.6) | copy-start | bytes 1572868
  1428.4 32.4 %all-to-all-start.1 = ((bf16[128,2,2048]{2,1,0:T(2,128)(2,1)}), bf16[128,2,2048]{2,1,0:T(2,128)(2,1)S(1)}, u32[]{:S(2)}, u32[]{:S(2)}) async-start(bf16[128,2,2048]{2,1,0:T(2,128)(2,1)} %reshape.409), calls=%async_computation.3 | async-start | bytes 2097152 | tf_op jit(solution)/shard_map/all_to_all | solution.py:103
  1466.9 7.0 copy-start.10
  1473.8 3.8 slice-start
  1476.2 2.2 slice-start.1
  1476.6 1.8 copy-start.4
Sparse Core Ops, SparseCore 0:
  46.7 639.6 reduce-scatter.2
  791.6 631.5 reduce-scatter.4
